TPU v7x, 32 devices: a whole 2x2x4 slice. The times are simulated.
32 devices in a mesh: groups: 2 (over x), user: 2 (over core), hist: 8 (over z, y).
Axes of the slice: x: 2, y: 2, z: 4, core: 2. Of those that a mesh axis runs over, the one named last changes fastest.
Arguments:
- item_table: bfloat16 [512, 1024], P('hist')
- item_ids: int32 [4, 512], P(('groups', 'user'), 'hist'), parts along dimension 0, may hold values from 0 to 511
- candidate_counts: int32 [4], P(('groups', 'user')), parts along dimension 0, may hold values from 256 to 512, as said below
- domain_ids: int32 [4, 512], P(('groups', 'user'), 'hist'), parts along dimension 0, may hold values from 0 to 1, as said below
- history_lengths: int32 [4], P(('groups', 'user')), parts along dimension 0, may hold values from 2048 to 4096, as said below
- history_keys: bfloat16 [4, 4096, 1024], P(('groups', 'user'), 'hist'), parts along dimension 0, may hold values from -9 to 9
- history_values: bfloat16 [4, 4096, 1024], P(('groups', 'user'), 'hist'), parts along dimension 0
- w_query: bfloat16 [1024, 1024], replicated, may hold values from -0.1875 to 0.1875
- w_gate: bfloat16 [1024, 1024], replicated, may hold values from -0.1875 to 0.1875
- w_out: bfloat16 [1024, 1024], replicated, may hold values from -0.1875 to 0.1875
- attn_gain: float32 [1024], replicated, may hold values from 0.1 to 1.9
- expert_weights: bfloat16 [2, 2, 1024, 1024], P('user'), may hold values from -0.1875 to 0.1875
Outputs:
- candidate_states: bfloat16 [4, 512, 1024], P(('groups', 'user'), 'hist'), parts along dimension 0
There are 2 independent parts, one for each index of `groups`. A program takes and returns all parts, laid end to end along the dimension named above; an argument that names none is the same for every part. Nothing has to cross between parts.
Inputs may be any that keep to these rules, and one draw needn't show every extreme that they name: `candidate_counts`: slots at or past a user's count are padding; some user has 512. `history_lengths`: positions at or past a user's length are not attended; some user has 4096. `domain_ids`: in each aligned block of 64 slots of a user, at most 48 slots name one domain; in the first block of every user exactly 48 name the same domain.
All inputs are finite; a program needn't handle non-finite values.
Results may differ from a plain program's by a relative error of at most 0.0059.
Values may be sent and summed in bfloat16 or wider, within the bound.
A program may use at most 64 MiB of HBM per device.

v0:
```python
import functools

import jax
import jax.numpy as jnp
from jax import lax
from jax.experimental import pallas as pl
from jax.experimental.pallas import tpu as pltpu
from jax.sharding import PartitionSpec as P

H = 8
CHUNKS = 2
norm_eps = 1e-05
MESH = pl.DeviceIdType.MESH


def rms_scale(matrix):
    return matrix * lax.rsqrt(jnp.mean(matrix * matrix, axis=-1, keepdims=True) + norm_eps)


def silu(value):
    half = value * 0.5
    return half + half * jnp.tanh(half)


def dot(left, right):
    return jnp.dot(left, right, preferred_element_type=jnp.float32)


def kernel(
    pairs,
    table,
    ids,
    counts,
    domains,
    lengths,
    keys,
    values,
    w_query,
    w_gate,
    w_out,
    gain,
    experts,
    out,
    rows,
    item_queries,
    key_buf,
    value_buf,
    query_w,
    gate_w,
    out_w,
    expert_w,
    id_buf,
    partial,
    pair_recv,
    z_send,
    z_recv,
    local_sem,
    table_zs,
    table_zr,
    table_ys,
    table_yr,
    table_ss,
    table_sr,
    id_zs,
    id_zr,
    id_ys,
    id_yr,
    expert_s,
    expert_r,
    sum_ys,
    sum_yr,
    sum_zs,
    sum_zr,
):
    me = lax.axis_index("hist")
    user = lax.axis_index("user")
    upper = lax.div(me, 2)
    lower = lax.rem(me, 2)
    slots = ids.shape[1]
    shard, width = table.shape
    items = rows.shape[0]
    half = shard // 2
    key_count = key_buf.shape[0]
    layers = experts.shape[1]
    head = width // H

    def peer(step):
        return lax.rem(upper + step, pairs) * 2 + lower

    other = upper * 2 + (1 - lower)
    to_pair = {"hist": other}
    to_sibling = {"user": 1 - user}

    def remote(src, dst, send, recv, target):
        return pltpu.make_async_remote_copy(
            src_ref=src,
            dst_ref=dst,
            send_sem=send,
            recv_sem=recv,
            device_id=target,
            device_id_type=MESH,
        )

    def half_rows(owner, core):
        start = pl.multiple_of(owner * shard + core * half, half)
        return rows.at[pl.ds(start, half)]

    own_rows = rows.at[pl.ds(pl.multiple_of(me * shard, shard), shard)]
    loads = [
        pltpu.make_async_copy(table, own_rows, local_sem.at[0]),
        pltpu.make_async_copy(w_query, query_w, local_sem.at[1]),
        pltpu.make_async_copy(keys.at[0], key_buf, local_sem.at[2]),
        pltpu.make_async_copy(values.at[0], value_buf, local_sem.at[3]),
        pltpu.make_async_copy(w_gate, gate_w, local_sem.at[4]),
        pltpu.make_async_copy(w_out, out_w, local_sem.at[5]),
        pltpu.make_async_copy(experts.at[0], expert_w.at[user], local_sem.at[6]),
    ]
    for load in loads:
        load.start()

    id_tile = id_buf.at[lower, upper]
    id_tile[...] = jnp.zeros(id_tile.shape, jnp.int32)
    id_tile[0:1, 0:slots] = ids[...]

    barrier = pltpu.get_barrier_semaphore()
    pl.semaphore_signal(barrier, inc=1, device_id=to_pair, device_id_type=MESH)
    pl.semaphore_signal(barrier, inc=1, device_id=to_sibling, device_id_type=MESH)

    @pl.loop(1, pairs)
    def _(step):
        pl.semaphore_signal(barrier, inc=1, device_id={"hist": peer(step)}, device_id_type=MESH)

    pl.semaphore_wait(barrier, pairs + 1)

    my_half = table.at[pl.ds(pl.multiple_of(user * half, half), half)]

    def id_z(step):
        return remote(id_tile, id_tile, id_zs.at[step], id_zr.at[step], {"hist": peer(step)})

    def id_z_arrival(step):
        source = lax.rem(upper - step + pairs, pairs)
        tile = id_buf.at[lower, source]
        return remote(tile, tile, id_zs.at[step], id_zr.at[step], {"hist": peer(step)})

    def table_z(step):
        return remote(
            my_half,
            half_rows(me, user),
            table_zs.at[step],
            table_zr.at[step],
            {"hist": peer(step)},
        )

    def source_at(step):
        return lax.rem(upper - step + pairs, pairs)

    def table_z_arrival(step):
        block = half_rows(source_at(step) * 2 + lower, user)
        return remote(
            block, block, table_zs.at[step], table_zr.at[step], {"hist": peer(step)}
        )

    def table_y(step, owner_low):
        block = half_rows(source_at(step) * 2 + owner_low, user)
        return remote(block, block, table_ys.at[step], table_yr.at[step], to_pair)

    def table_s(step, owner_low, core):
        block = half_rows(source_at(step) * 2 + owner_low, core)
        slot = 2 * step + jnp.where(owner_low == lower, 0, 1)
        return remote(block, block, table_ss.at[slot], table_sr.at[slot], to_sibling)

    @pl.loop(1, pairs)
    def _(step):
        table_z(step).start()

    table_y_first = remote(
        my_half, half_rows(me, user), table_ys.at[0], table_yr.at[0], to_pair
    )
    table_y_first.start()

    @pl.loop(1, pairs)
    def _(step):
        id_z(step).start()

    expert_copy = remote(experts.at[0], expert_w.at[user], expert_s, expert_r, to_sibling)
    expert_copy.start()

    def project(step):
        start = pl.multiple_of(source_at(step) * 2 * shard, 2 * shard)
        block = rows[pl.ds(start, 2 * shard), :].astype(jnp.float32)
        normed = rms_scale(block).astype(jnp.bfloat16)
        item_queries[pl.ds(start, 2 * shard), :] = dot(normed, query_w[...]).astype(jnp.bfloat16)

    table_y(0, 1 - lower).wait_recv()
    table_s(0, 1 - lower, user).start()
    loads[0].wait()
    loads[1].wait()

    @pl.loop(1, pairs)
    def _(step):
        table_z_arrival(step).wait_recv()
        table_y(step, lower).start()
        table_s(step, lower, user).start()

    @pl.loop(1, pairs)
    def _(step):
        id_z_arrival(step).wait_recv()

    id_y = remote(id_buf.at[lower], id_buf.at[lower], id_ys, id_yr, to_pair)
    id_y.start()

    @pl.loop(1, pairs)
    def _(step):
        table_y(step, 1 - lower).wait_recv()
        table_s(step, 1 - lower, user).start()
        previous = step - 1

        @pl.when(previous > 0)
        def _():
            table_s(previous, lower, 1 - user).wait_recv()

        table_s(previous, 1 - lower, 1 - user).wait_recv()
        project(previous)

    loads[2].wait()
    loads[3].wait()
    position = me * key_count + lax.broadcasted_iota(jnp.int32, (key_count, width), 0)
    value_buf[...] = jnp.where(position < lengths[0], value_buf[...], jnp.zeros((), jnp.bfloat16))
    table_s(pairs - 1, lower, 1 - user).wait_recv()
    table_s(pairs - 1, 1 - lower, 1 - user).wait_recv()
    project(pairs - 1)
    remote(
        id_buf.at[1 - lower], id_buf.at[1 - lower], id_ys, id_yr, to_pair
    ).wait_recv()

    lane_count = id_buf.shape[-1]
    eye = lax.broadcasted_iota(jnp.int32, (slots, lane_count), 0) == lax.broadcasted_iota(
        jnp.int32, (slots, lane_count), 1
    )

    def column(row):
        return jnp.sum(jnp.where(eye, row.astype(jnp.float32), 0.0), axis=1, keepdims=True)

    item_lane = lax.broadcasted_iota(jnp.int32, (slots, items), 1).astype(jnp.float32)

    def onehot(low, up):
        tile = id_buf[low, up]
        return jnp.where(item_lane == column(tile[0:1, :]), 1.0, 0.0).astype(jnp.bfloat16)

    turns = pairs * CHUNKS
    part = width // CHUNKS
    quads = pairs // 2
    quad = lax.div(upper, 2)
    side = lax.rem(upper, 2)

    def group_of(turn):
        return lax.rem(lax.div(turn, 2 * CHUNKS) + 1, quads)

    def near_of(turn):
        return lax.rem(lax.div(turn, CHUNKS), 2)

    def attend(turn):
        near = near_of(turn)
        chunk = lax.rem(turn, CHUNKS)
        target_side = near * side + (1 - near) * (1 - side)
        target = lax.rem(quad + group_of(turn), quads) * 2 + target_side
        chosen = jnp.concatenate([onehot(0, target), onehot(1, target)], axis=0)
        first = pl.multiple_of(chunk * part, part)
        queries = dot(chosen, item_queries[:, pl.ds(first, part)]).astype(jnp.bfloat16)
        for number in range(H // CHUNKS):
            cols = slice(number * head, (number + 1) * head)
            source = pl.ds(pl.multiple_of(first + number * head, head), head)
            scores = lax.dot_general(
                queries[:, cols],
                key_buf[:, source],
                (((1,), (1,)), ((), ())),
                preferred_element_type=jnp.float32,
            )
            halved = scores * (0.5 * head ** (-0.5))
            weights = (halved + halved * jnp.tanh(halved)).astype(jnp.bfloat16)
            mixed = dot(weights, value_buf[:, source]).astype(jnp.bfloat16)
            partial[turn, 0, :, cols] = mixed[:slots]
            partial[turn, 1, :, cols] = mixed[slots:]

    def sum_y(turn):
        return remote(
            partial.at[turn, 1 - lower],
            pair_recv.at[turn],
            sum_ys.at[turn],
            sum_yr.at[turn],
            to_pair,
        )

    def sum_z(turn):
        near = near_of(turn)
        across = lax.rem(quad + group_of(turn), quads) * 2 + side
        beside = quad * 2 + (1 - side)
        reached = near * across + (1 - near) * beside
        return remote(
            z_send.at[turn],
            z_recv.at[turn],
            sum_zs.at[turn],
            sum_zr.at[turn],
            {"hist": reached * 2 + lower},
        )

    def pair_sum(turn):
        sum_y(turn).wait_recv()
        return partial[turn, lower].astype(jnp.float32) + pair_recv[turn].astype(jnp.float32)

    def arrived_sum(turn):
        sum_z(turn).wait_recv()
        return z_recv[turn].astype(jnp.float32)

    def pass_on(turn):
        near = near_of(turn)

        @pl.when(near == 0)
        def _():
            z_send[turn] = pair_sum(turn).astype(jnp.bfloat16)

        @pl.when(near == 1)
        def _():
            z_send[turn] = (pair_sum(turn) + arrived_sum(turn - CHUNKS)).astype(jnp.bfloat16)

        sum_z(turn).start()

    @pl.loop(0, turns)
    def _(turn):
        attend(turn)
        sum_y(turn).start()

        @pl.when((turn > 0) & (turn <= turns - CHUNKS))
        def _():
            pass_on(turn - 1)

    loads[4].wait()
    loads[5].wait()
    embedded = dot(onehot(lower, upper), rows[...])
    normed = rms_scale(embedded).astype(jnp.bfloat16)
    gating = silu(dot(normed, gate_w[...])) * gain[...]

    sums = []
    for chunk in range(CHUNKS):
        last = turns - CHUNKS + chunk
        total = pair_sum(last) + arrived_sum(last - CHUNKS)

        def gather_sum(group, total, chunk=chunk):
            return total + arrived_sum((2 * group - 1) * CHUNKS + chunk)

        sums.append(lax.fori_loop(1, quads, gather_sum, total))
    attended = jnp.concatenate(sums, axis=1)
    gated = (rms_scale(attended) * gating).astype(jnp.bfloat16)
    state = (embedded + dot(gated, out_w[...])).astype(jnp.bfloat16)
    loads[6].wait()
    remote(
        experts.at[0], expert_w.at[1 - user], expert_s, expert_r, to_sibling
    ).wait_recv()

    results = []
    for expert in range(expert_w.shape[0]):
        current = state
        for layer in range(layers):
            lifted = dot(current, expert_w[expert, layer])
            current = (current.astype(jnp.float32) + silu(lifted)).astype(jnp.bfloat16)
        results.append(current)
    padded_domain = jnp.concatenate(
        [domains[...], jnp.zeros((1, lane_count - slots), jnp.int32)], axis=1
    )
    domain = column(padded_domain)
    picked = results[0].astype(jnp.float32)
    for expert in range(1, len(results)):
        picked = jnp.where(domain == expert, results[expert].astype(jnp.float32), picked)
    slot = me * slots + lax.broadcasted_iota(jnp.int32, (slots, 1), 0)
    out[0] = jnp.where(slot < counts[0], picked, 0.0).astype(jnp.bfloat16)

    expert_copy.wait_send()
    table_y_first.wait_send()
    table_s(0, 1 - lower, user).wait_send()
    id_y.wait_send()

    @pl.loop(1, pairs)
    def _(step):
        id_z(step).wait_send()
        table_z(step).wait_send()
        table_y(step, lower).wait_send()
        table_s(step, lower, user).wait_send()
        table_s(step, 1 - lower, user).wait_send()

    @pl.loop(0, turns)
    def _(turn):
        sum_y(turn).wait_send()

    @pl.loop(0, turns - CHUNKS)
    def _(turn):
        sum_z(turn).wait_send()


def on_device(
    item_table,
    item_ids,
    candidate_counts,
    domain_ids,
    history_lengths,
    history_keys,
    history_values,
    w_query,
    w_gate,
    w_out,
    attn_gain,
    expert_weights,
):
    slots = item_ids.shape[1]
    shard, width = item_table.shape
    hist = lax.axis_size("hist")
    users = lax.axis_size("user")
    pairs = hist // 2
    turns = pairs * CHUNKS
    part = width // CHUNKS
    key_count = history_keys.shape[1]
    layers = expert_weights.shape[1]
    bf16 = jnp.bfloat16
    dma = pltpu.SemaphoreType.DMA
    anywhere = pl.BlockSpec(memory_space=pl.ANY)
    vmem = pl.BlockSpec(memory_space=pltpu.VMEM)
    smem = pl.BlockSpec(memory_space=pltpu.SMEM)
    lanes = 128 * ((slots + 127) // 128)
    return pl.pallas_call(
        functools.partial(kernel, pairs),
        out_shape=jax.ShapeDtypeStruct((1, slots, width), bf16),
        in_specs=[
            anywhere,
            vmem,
            smem,
            vmem,
            smem,
            anywhere,
            anywhere,
            anywhere,
            anywhere,
            anywhere,
            vmem,
            anywhere,
        ],
        out_specs=vmem,
        scratch_shapes=[
            pltpu.VMEM((hist * shard, width), bf16),
            pltpu.VMEM((hist * shard, width), bf16),
            pltpu.VMEM((key_count, width), bf16),
            pltpu.VMEM((key_count, width), bf16),
            pltpu.VMEM(w_query.shape, bf16),
            pltpu.VMEM(w_gate.shape, bf16),
            pltpu.VMEM(w_out.shape, bf16),
            pltpu.VMEM((users, layers, width, width), bf16),
            pltpu.VMEM((2, pairs, 8, lanes), jnp.int32),
            pltpu.VMEM((turns, 2, slots, part), bf16),
            pltpu.VMEM((turns, slots, part), bf16),
            pltpu.VMEM((turns, slots, part), bf16),
            pltpu.VMEM((turns, slots, part), bf16),
            dma((7,)),
            dma((pairs,)),
            dma((pairs,)),
            dma((pairs,)),
            dma((pairs,)),
            dma((2 * pairs,)),
            dma((2 * pairs,)),
            dma((pairs,)),
            dma((pairs,)),
            dma,
            dma,
            dma,
            dma,
            dma((turns,)),
            dma((turns,)),
            dma((turns,)),
            dma((turns,)),
        ],
        compiler_params=pltpu.CompilerParams(
            collective_id=0, has_side_effects=True, vmem_limit_bytes=60 * 1024 * 1024
        ),
    )(
        item_table,
        item_ids,
        candidate_counts,
        domain_ids,
        history_lengths,
        history_keys,
        history_values,
        w_query,
        w_gate,
        w_out,
        attn_gain.reshape(1, width),
        expert_weights,
    )


def solution(mesh):
    in_specs = (
        P("hist", None),
        P(("groups", "user"), "hist"),
        P(("groups", "user")),
        P(("groups", "user"), "hist"),
        P(("groups", "user")),
        P(("groups", "user"), "hist", None),
        P(("groups", "user"), "hist", None),
        P(),
        P(),
        P(),
        P(),
        P("user", None, None, None),
    )
    out_specs = P(("groups", "user"), "hist", None)
    return jax.shard_map(
        on_device, mesh=mesh, in_specs=in_specs, out_specs=out_specs, check_vma=False
    )
```

profile of v0, /device:TPU:0, one launch (start us, length us, event | category | flops | bytes accessed | tf_op | source)
XLA Modules:
  0.0 44.3 jit_solution(6936904583568891989)
XLA Ops:
  1.3 41.4 %shard_map.118 = bf16[1,64,1024]{2,1,0:T(8,128)(2,1)} custom-call(bf16[64,1024]{1,0:T(8,128)(2,1)} %table.1, s32[1,64]{1,0:T(1,128)} %ids.1, s32[1]{0:T(128)S(6)} %copy.14.counts, s32[1,64]{1,0:T(1,128)} %domains.1, s32[1]{0:T(128)S(6)} %copy.15.lengths, bf16[1,512,1024]{2,1,0:T(8,128)(2,1)} %keys.1, bf16[1,512,1024]{2,1,0:T(8,128)(2,1)} %values.1, ...), custom_call_target="tpu_custom_call" | custom-call | tf_op jit(solution)/shard_map/pallas_call | solution.py:428
  42.7 1.6 %copy.16 = bf16[1,64,1024]{2,1,0:T(8,128)(2,1)} copy(bf16[1,64,1024]{2,1,0:T(8,128)(2,1)} %shard_map.118) | data formatting | bytes 262144
where the time goes:
time: 44.5 us; the launch traced here: 44.3 us
  Pallas kernels  41.4 us (93%)
  local copies, waits for them, and re-layouts  1.57 us (4%)
  between operations  1.3 us (3%)
    pallas_call x1, Pallas kernels, on_device(): pl.pallas_call(functools.partial(kernel, pairs), out_shape=jax.ShapeDtype...  41.4 us
    unnamed x1, local copies, waits for them, and re-layouts  1.57 us

commit v1 on v0

--- a/solution.py
+++ b/solution.py
@@ -9,6 +9,7 @@
 
 H = 8
 CHUNKS = 2
+LAG = 3
 norm_eps = 1e-05
 MESH = pl.DeviceIdType.MESH
 
@@ -54,6 +55,11 @@
     pair_recv,
     z_send,
     z_recv,
+    id_in,
+    domain_in,
+    gain_in,
+    count_in,
+    length_in,
     local_sem,
     table_zs,
     table_zr,
@@ -77,6 +83,18 @@
     upper = lax.div(me, 2)
     lower = lax.rem(me, 2)
     slots = ids.shape[1]
+
+    barrier = pltpu.get_barrier_semaphore()
+    pl.semaphore_signal(
+        barrier, inc=1, device_id={"hist": upper * 2 + (1 - lower)}, device_id_type=MESH
+    )
+    pl.semaphore_signal(barrier, inc=1, device_id={"user": 1 - user}, device_id_type=MESH)
+
+    @pl.loop(1, pairs)
+    def _(step):
+        there = lax.rem(upper + step, pairs) * 2 + lower
+        pl.semaphore_signal(barrier, inc=1, device_id={"hist": there}, device_id_type=MESH)
+
     shard, width = table.shape
     items = rows.shape[0]
     half = shard // 2
@@ -115,21 +133,24 @@
         pltpu.make_async_copy(w_out, out_w, local_sem.at[5]),
         pltpu.make_async_copy(experts.at[0], expert_w.at[user], local_sem.at[6]),
     ]
+    id_load = pltpu.make_async_copy(ids, id_in, local_sem.at[7])
+    id_load.start()
     for load in loads:
         load.start()
 
+    small = [
+        pltpu.make_async_copy(counts, count_in, local_sem.at[8]),
+        pltpu.make_async_copy(lengths, length_in, local_sem.at[9]),
+        pltpu.make_async_copy(domains, domain_in, local_sem.at[10]),
+        pltpu.make_async_copy(gain, gain_in, local_sem.at[11]),
+    ]
+    for load in small:
+        load.start()
+
+    id_load.wait()
     id_tile = id_buf.at[lower, upper]
     id_tile[...] = jnp.zeros(id_tile.shape, jnp.int32)
-    id_tile[0:1, 0:slots] = ids[...]
-
-    barrier = pltpu.get_barrier_semaphore()
-    pl.semaphore_signal(barrier, inc=1, device_id=to_pair, device_id_type=MESH)
-    pl.semaphore_signal(barrier, inc=1, device_id=to_sibling, device_id_type=MESH)
-
-    @pl.loop(1, pairs)
-    def _(step):
-        pl.semaphore_signal(barrier, inc=1, device_id={"hist": peer(step)}, device_id_type=MESH)
-
+    id_tile[0:1, 0:slots] = id_in[...]
     pl.semaphore_wait(barrier, pairs + 1)
 
     my_half = table.at[pl.ds(pl.multiple_of(user * half, half), half)]
@@ -224,8 +245,10 @@
 
     loads[2].wait()
     loads[3].wait()
+    small[0].wait()
+    small[1].wait()
     position = me * key_count + lax.broadcasted_iota(jnp.int32, (key_count, width), 0)
-    value_buf[...] = jnp.where(position < lengths[0], value_buf[...], jnp.zeros((), jnp.bfloat16))
+    value_buf[...] = jnp.where(position < length_in[...], value_buf[...], jnp.zeros((), jnp.bfloat16))
     table_s(pairs - 1, lower, 1 - user).wait_recv()
     table_s(pairs - 1, 1 - lower, 1 - user).wait_recv()
     project(pairs - 1)
@@ -330,15 +353,23 @@
         attend(turn)
         sum_y(turn).start()
 
-        @pl.when((turn > 0) & (turn <= turns - CHUNKS))
+        @pl.when((turn >= LAG) & (turn < turns - CHUNKS + LAG))
         def _():
-            pass_on(turn - 1)
+            pass_on(turn - LAG)
+
+    if LAG > CHUNKS:
+
+        @pl.loop(turns - LAG, turns - CHUNKS)
+        def _(turn):
+            pass_on(turn)
 
     loads[4].wait()
     loads[5].wait()
+    small[2].wait()
+    small[3].wait()
     embedded = dot(onehot(lower, upper), rows[...])
     normed = rms_scale(embedded).astype(jnp.bfloat16)
-    gating = silu(dot(normed, gate_w[...])) * gain[...]
+    gating = silu(dot(normed, gate_w[...])) * gain_in[...]
 
     sums = []
     for chunk in range(CHUNKS):
@@ -365,14 +396,14 @@
             current = (current.astype(jnp.float32) + silu(lifted)).astype(jnp.bfloat16)
         results.append(current)
     padded_domain = jnp.concatenate(
-        [domains[...], jnp.zeros((1, lane_count - slots), jnp.int32)], axis=1
+        [domain_in[...], jnp.zeros((1, lane_count - slots), jnp.int32)], axis=1
     )
     domain = column(padded_domain)
     picked = results[0].astype(jnp.float32)
     for expert in range(1, len(results)):
         picked = jnp.where(domain == expert, results[expert].astype(jnp.float32), picked)
     slot = me * slots + lax.broadcasted_iota(jnp.int32, (slots, 1), 0)
-    out[0] = jnp.where(slot < counts[0], picked, 0.0).astype(jnp.bfloat16)
+    out[0] = jnp.where(slot < count_in[...], picked, 0.0).astype(jnp.bfloat16)
 
     expert_copy.wait_send()
     table_y_first.wait_send()
@@ -421,27 +452,13 @@
     layers = expert_weights.shape[1]
     bf16 = jnp.bfloat16
     dma = pltpu.SemaphoreType.DMA
-    anywhere = pl.BlockSpec(memory_space=pl.ANY)
+    anywhere = pl.BlockSpec(memory_space=pltpu.HBM)
     vmem = pl.BlockSpec(memory_space=pltpu.VMEM)
-    smem = pl.BlockSpec(memory_space=pltpu.SMEM)
     lanes = 128 * ((slots + 127) // 128)
     return pl.pallas_call(
         functools.partial(kernel, pairs),
-        out_shape=jax.ShapeDtypeStruct((1, slots, width), bf16),
-        in_specs=[
-            anywhere,
-            vmem,
-            smem,
-            vmem,
-            smem,
-            anywhere,
-            anywhere,
-            anywhere,
-            anywhere,
-            anywhere,
-            vmem,
-            anywhere,
-        ],
+        out_shape=pltpu.VMEM((1, slots, width), bf16),
+        in_specs=[anywhere] * 12,
         out_specs=vmem,
         scratch_shapes=[
             pltpu.VMEM((hist * shard, width), bf16),
@@ -457,7 +474,12 @@
             pltpu.VMEM((turns, slots, part), bf16),
             pltpu.VMEM((turns, slots, part), bf16),
             pltpu.VMEM((turns, slots, part), bf16),
-            dma((7,)),
+            pltpu.VMEM((1, slots), jnp.int32),
+            pltpu.VMEM((1, slots), jnp.int32),
+            pltpu.VMEM((1, width), jnp.float32),
+            pltpu.VMEM((1, 1), jnp.int32),
+            pltpu.VMEM((1, 1), jnp.int32),
+            dma((12,)),
             dma((pairs,)),
             dma((pairs,)),
             dma((pairs,)),
@@ -481,9 +503,9 @@
     )(
         item_table,
         item_ids,
-        candidate_counts,
+        candidate_counts.reshape(1, 1),
         domain_ids,
-        history_lengths,
+        history_lengths.reshape(1, 1),
         history_keys,
         history_values,
         w_query,

time: 44.5 us -> 40.2 us (0.903)
  Pallas kernels: 41.4 us -> 38.1 us
  local copies, waits for them, and re-layouts: 1.57 us -> 0.66 us
    pallas_call x1, Pallas kernels: 41.4 us -> 38.1 us  [on_device(): pl.pallas_call(functools.partial(kernel, pairs), out_shape=pltpu.VMEM((1,...]
    unnamed x1, local copies, waits for them, and re-layouts: 1.57 us -> 0.66 us
where the time goes in v1:
time: 40.2 us; the launch traced here: 40 us
  Pallas kernels  38.1 us (95%)
  between operations  1.3 us (3%)
  local copies, waits for them, and re-layouts  0.66 us (2%)
    pallas_call x1, Pallas kernels, on_device(): pl.pallas_call(functools.partial(kernel, pairs), out_shape=pltpu.VMEM((1,...  38.1 us

profile of v1, /device:TPU:0, one launch (start us, length us, event | category | flops | bytes accessed | tf_op | source)
XLA Modules:
  0.0 40.0 jit_solution(630732816961608453)
XLA Ops:
  1.3 38.1 %shard_map.118 = bf16[1,64,1024]{2,1,0:T(8,128)(2,1)S(1)} custom-call(bf16[64,1024]{1,0:T(8,128)(2,1)} %table.1, s32[1,64]{1,0:T(1,128)} %ids.1, s32[1,1]{1,0:T(1,128)} %bitcast.3.counts, s32[1,64]{1,0:T(1,128)} %domains.1, s32[1,1]{1,0:T(1,128)} %bitcast.4.lengths, bf16[1,512,1024]{2,1,0:T(8,128)(2,1)} %keys.1, bf16[1,512,1024]{2,1,0:T(8,128)(2,1)} %values.1, ...), custom_call_target="tpu_custom_call" | custom-call | tf_op jit(solution)/shard_map/pallas_call | solution.py:458
  39.4 0.7 %copy.14 = bf16[1,64,1024]{2,1,0:T(8,128)(2,1)} copy(bf16[1,64,1024]{2,1,0:T(8,128)(2,1)S(1)} %shard_map.118) | data formatting | bytes 262144

commit v2 on v1

--- a/solution.py
+++ b/solution.py
@@ -9,7 +9,7 @@
 
 H = 8
 CHUNKS = 2
-LAG = 3
+LAG = 2
 norm_eps = 1e-05
 MESH = pl.DeviceIdType.MESH
 
@@ -102,8 +102,12 @@
     layers = experts.shape[1]
     head = width // H
 
-    def peer(step):
-        return lax.rem(upper + step, pairs) * 2 + lower
+    margin = jnp.minimum(upper, pairs - 1 - upper)
+    toward = jnp.where(2 * upper < pairs, 1, -1)
+
+    def near_peer(step):
+        away = lax.div(step + 1, 2) * (2 * lax.rem(step, 2) - 1)
+        return upper + jnp.where(step <= 2 * margin, away, toward * (step - margin))
 
     other = upper * 2 + (1 - lower)
     to_pair = {"hist": other}
@@ -135,8 +139,8 @@
     ]
     id_load = pltpu.make_async_copy(ids, id_in, local_sem.at[7])
     id_load.start()
-    for load in loads:
-        load.start()
+    loads[0].start()
+    loads[1].start()
 
     small = [
         pltpu.make_async_copy(counts, count_in, local_sem.at[8]),
@@ -144,117 +148,114 @@
         pltpu.make_async_copy(domains, domain_in, local_sem.at[10]),
         pltpu.make_async_copy(gain, gain_in, local_sem.at[11]),
     ]
-    for load in small:
-        load.start()
-
     id_load.wait()
     id_tile = id_buf.at[lower, upper]
     id_tile[...] = jnp.zeros(id_tile.shape, jnp.int32)
     id_tile[0:1, 0:slots] = id_in[...]
     pl.semaphore_wait(barrier, pairs + 1)
 
-    my_half = table.at[pl.ds(pl.multiple_of(user * half, half), half)]
-
-    def id_z(step):
-        return remote(id_tile, id_tile, id_zs.at[step], id_zr.at[step], {"hist": peer(step)})
-
-    def id_z_arrival(step):
-        source = lax.rem(upper - step + pairs, pairs)
+    loads[0].wait()
+    my_half = half_rows(me, user)
+
+    def id_z(source, there):
         tile = id_buf.at[lower, source]
-        return remote(tile, tile, id_zs.at[step], id_zr.at[step], {"hist": peer(step)})
-
-    def table_z(step):
+        return remote(tile, tile, id_zs, id_zr.at[source], {"hist": there * 2 + lower})
+
+    def table_z(source, there):
+        block = half_rows(source * 2 + lower, user)
         return remote(
-            my_half,
-            half_rows(me, user),
-            table_zs.at[step],
-            table_zr.at[step],
-            {"hist": peer(step)},
+            block, block, table_zs, table_zr.at[source], {"hist": there * 2 + lower}
         )
 
-    def source_at(step):
-        return lax.rem(upper - step + pairs, pairs)
-
-    def table_z_arrival(step):
-        block = half_rows(source_at(step) * 2 + lower, user)
-        return remote(
-            block, block, table_zs.at[step], table_zr.at[step], {"hist": peer(step)}
-        )
-
-    def table_y(step, owner_low):
-        block = half_rows(source_at(step) * 2 + owner_low, user)
-        return remote(block, block, table_ys.at[step], table_yr.at[step], to_pair)
-
-    def table_s(step, owner_low, core):
-        block = half_rows(source_at(step) * 2 + owner_low, core)
-        slot = 2 * step + jnp.where(owner_low == lower, 0, 1)
-        return remote(block, block, table_ss.at[slot], table_sr.at[slot], to_sibling)
+    def table_y(source, owner_low):
+        block = half_rows(source * 2 + owner_low, user)
+        return remote(block, block, table_ys, table_yr.at[source], to_pair)
+
+    def table_s(source, owner_low, core):
+        block = half_rows(source * 2 + owner_low, core)
+        slot = 2 * source + jnp.where(owner_low == lower, 0, 1)
+        return remote(block, block, table_ss, table_sr.at[slot], to_sibling)
+
+    table_y(upper, lower).start()
 
     @pl.loop(1, pairs)
     def _(step):
-        table_z(step).start()
-
-    table_y_first = remote(
-        my_half, half_rows(me, user), table_ys.at[0], table_yr.at[0], to_pair
-    )
-    table_y_first.start()
+        table_z(upper, near_peer(step)).start()
 
     @pl.loop(1, pairs)
     def _(step):
-        id_z(step).start()
-
-    expert_copy = remote(experts.at[0], expert_w.at[user], expert_s, expert_r, to_sibling)
-    expert_copy.start()
-
-    def project(step):
-        start = pl.multiple_of(source_at(step) * 2 * shard, 2 * shard)
+        id_z(upper, near_peer(step)).start()
+
+    loads[2].start()
+    loads[3].start()
+    for load in small:
+        load.start()
+
+    def project(source):
+        start = pl.multiple_of(source * 2 * shard, 2 * shard)
         block = rows[pl.ds(start, 2 * shard), :].astype(jnp.float32)
         normed = rms_scale(block).astype(jnp.bfloat16)
         item_queries[pl.ds(start, 2 * shard), :] = dot(normed, query_w[...]).astype(jnp.bfloat16)
 
-    table_y(0, 1 - lower).wait_recv()
-    table_s(0, 1 - lower, user).start()
-    loads[0].wait()
+    def forward(step):
+        source = near_peer(step)
+        table_z(source, upper).wait_recv()
+        table_y(source, lower).start()
+        table_s(source, lower, user).start()
+
+    def finish(step):
+        source = near_peer(step)
+        table_y(source, 1 - lower).wait_recv()
+        table_s(source, 1 - lower, user).start()
+
+    def complete(source):
+        table_s(source, lower, 1 - user).wait_recv()
+        table_s(source, 1 - lower, 1 - user).wait_recv()
+
+    table_y(upper, 1 - lower).wait_recv()
+    table_s(upper, 1 - lower, user).start()
     loads[1].wait()
 
     @pl.loop(1, pairs)
     def _(step):
-        table_z_arrival(step).wait_recv()
-        table_y(step, lower).start()
-        table_s(step, lower, user).start()
-
-    @pl.loop(1, pairs)
-    def _(step):
-        id_z_arrival(step).wait_recv()
-
-    id_y = remote(id_buf.at[lower], id_buf.at[lower], id_ys, id_yr, to_pair)
-    id_y.start()
-
-    @pl.loop(1, pairs)
-    def _(step):
-        table_y(step, 1 - lower).wait_recv()
-        table_s(step, 1 - lower, user).start()
-        previous = step - 1
-
-        @pl.when(previous > 0)
-        def _():
-            table_s(previous, lower, 1 - user).wait_recv()
-
-        table_s(previous, 1 - lower, 1 - user).wait_recv()
-        project(previous)
+        forward(step)
 
     loads[2].wait()
     loads[3].wait()
     small[0].wait()
     small[1].wait()
     position = me * key_count + lax.broadcasted_iota(jnp.int32, (key_count, width), 0)
-    value_buf[...] = jnp.where(position < length_in[...], value_buf[...], jnp.zeros((), jnp.bfloat16))
-    table_s(pairs - 1, lower, 1 - user).wait_recv()
-    table_s(pairs - 1, 1 - lower, 1 - user).wait_recv()
-    project(pairs - 1)
+    value_buf[...] = jnp.where(
+        position < length_in[...], value_buf[...], jnp.zeros((), jnp.bfloat16)
+    )
+
+    @pl.loop(1, pairs)
+    def _(step):
+        id_z(near_peer(step), upper).wait_recv()
+
+    id_y = remote(id_buf.at[lower], id_buf.at[lower], id_ys, id_yr, to_pair)
+    id_y.start()
+    finish(1)
+    table_s(upper, 1 - lower, 1 - user).wait_recv()
+    project(upper)
+
+    @pl.loop(1, pairs)
+    def _(step):
+        @pl.when(step < pairs - 1)
+        def _():
+            finish(step + 1)
+
+        complete(near_peer(step))
+        project(near_peer(step))
+
     remote(
         id_buf.at[1 - lower], id_buf.at[1 - lower], id_ys, id_yr, to_pair
     ).wait_recv()
+    loads[4].start()
+    loads[5].start()
+    loads[6].start()
+    expert_copy = remote(experts.at[0], expert_w.at[user], expert_s, expert_r, to_sibling)
+    expert_copy.start()
 
     lane_count = id_buf.shape[-1]
     eye = lax.broadcasted_iota(jnp.int32, (slots, lane_count), 0) == lax.broadcasted_iota(
@@ -276,11 +277,13 @@
     quad = lax.div(upper, 2)
     side = lax.rem(upper, 2)
 
+    early = quads * CHUNKS
+
     def group_of(turn):
-        return lax.rem(lax.div(turn, 2 * CHUNKS) + 1, quads)
+        return lax.rem(lax.rem(lax.div(turn, CHUNKS), quads) + 1, quads)
 
     def near_of(turn):
-        return lax.rem(lax.div(turn, CHUNKS), 2)
+        return lax.div(turn, early)
 
     def attend(turn):
         near = near_of(turn)
@@ -309,7 +312,7 @@
         return remote(
             partial.at[turn, 1 - lower],
             pair_recv.at[turn],
-            sum_ys.at[turn],
+            sum_ys,
             sum_yr.at[turn],
             to_pair,
         )
@@ -322,7 +325,7 @@
         return remote(
             z_send.at[turn],
             z_recv.at[turn],
-            sum_zs.at[turn],
+            sum_zs,
             sum_zr.at[turn],
             {"hist": reached * 2 + lower},
         )
@@ -344,7 +347,7 @@
 
         @pl.when(near == 1)
         def _():
-            z_send[turn] = (pair_sum(turn) + arrived_sum(turn - CHUNKS)).astype(jnp.bfloat16)
+            z_send[turn] = (pair_sum(turn) + arrived_sum(turn - early)).astype(jnp.bfloat16)
 
         sum_z(turn).start()
 
@@ -371,13 +374,26 @@
     normed = rms_scale(embedded).astype(jnp.bfloat16)
     gating = silu(dot(normed, gate_w[...])) * gain_in[...]
 
+    expert_copy.wait_send()
+    id_y.wait_send()
+
+    def sent(count, sem):
+        block = rows.at[pl.ds(0, count * half)]
+        remote(block, block, sem, table_yr.at[0], to_pair).wait_send()
+
+    sent(pairs - 1, table_zs)
+    sent(pairs, table_ys)
+    sent(2 * pairs - 1, table_ss)
+    tiles = id_buf.at[0, pl.ds(0, pairs - 1)]
+    remote(tiles, tiles, id_zs, id_yr, to_pair).wait_send()
+
     sums = []
     for chunk in range(CHUNKS):
         last = turns - CHUNKS + chunk
-        total = pair_sum(last) + arrived_sum(last - CHUNKS)
+        total = pair_sum(last) + arrived_sum(last - early)
 
         def gather_sum(group, total, chunk=chunk):
-            return total + arrived_sum((2 * group - 1) * CHUNKS + chunk)
+            return total + arrived_sum((quads + group - 1) * CHUNKS + chunk)
 
         sums.append(lax.fori_loop(1, quads, gather_sum, total))
     attended = jnp.concatenate(sums, axis=1)
@@ -405,26 +421,9 @@
     slot = me * slots + lax.broadcasted_iota(jnp.int32, (slots, 1), 0)
     out[0] = jnp.where(slot < count_in[...], picked, 0.0).astype(jnp.bfloat16)
 
-    expert_copy.wait_send()
-    table_y_first.wait_send()
-    table_s(0, 1 - lower, user).wait_send()
-    id_y.wait_send()
-
-    @pl.loop(1, pairs)
-    def _(step):
-        id_z(step).wait_send()
-        table_z(step).wait_send()
-        table_y(step, lower).wait_send()
-        table_s(step, lower, user).wait_send()
-        table_s(step, 1 - lower, user).wait_send()
-
-    @pl.loop(0, turns)
-    def _(turn):
-        sum_y(turn).wait_send()
-
-    @pl.loop(0, turns - CHUNKS)
-    def _(turn):
-        sum_z(turn).wait_send()
+    remote(pair_recv, pair_recv, sum_ys, sum_yr.at[0], to_pair).wait_send()
+    sent_z = z_recv.at[pl.ds(0, turns - CHUNKS)]
+    remote(sent_z, sent_z, sum_zs, sum_zr.at[0], to_pair).wait_send()
 
 
 def on_device(
@@ -480,21 +479,21 @@
             pltpu.VMEM((1, 1), jnp.int32),
             pltpu.VMEM((1, 1), jnp.int32),
             dma((12,)),
+            dma,
             dma((pairs,)),
+            dma,
             dma((pairs,)),
+            dma,
+            dma((2 * pairs,)),
+            dma,
             dma((pairs,)),
-            dma((pairs,)),
-            dma((2 * pairs,)),
-            dma((2 * pairs,)),
-            dma((pairs,)),
-            dma((pairs,)),
+            dma,
             dma,
             dma,
             dma,
             dma,
             dma((turns,)),
-            dma((turns,)),
-            dma((turns,)),
+            dma,
             dma((turns,)),
         ],
         compiler_params=pltpu.CompilerParams(

time: 40.2 us -> 37.8 us (0.940)
  Pallas kernels: 38.1 us -> 35.7 us
    pallas_call x1, Pallas kernels: 38.1 us -> 35.7 us  [on_device(): pl.pallas_call(functools.partial(kernel, pairs), out_shape=pltpu.VMEM((1,...]
where the time goes in v2:
time: 37.8 us; the launch traced here: 37.6 us
  Pallas kernels  35.7 us (94%)
  between operations  1.3 us (3%)
  local copies, waits for them, and re-layouts  0.66 us (2%)
    pallas_call x1, Pallas kernels, on_device(): pl.pallas_call(functools.partial(kernel, pairs), out_shape=pltpu.VMEM((1,...  35.7 us

profile of v2, /device:TPU:0, one launch (start us, length us, event | category | flops | bytes accessed | tf_op | source)
XLA Modules:
  0.0 37.6 jit_solution(5473848243530212303)
XLA Ops:
  1.3 35.7 %shard_map.118 = bf16[1,64,1024]{2,1,0:T(8,128)(2,1)S(1)} custom-call(bf16[64,1024]{1,0:T(8,128)(2,1)} %table.1, s32[1,64]{1,0:T(1,128)} %ids.1, s32[1,1]{1,0:T(1,128)} %bitcast.3.counts, s32[1,64]{1,0:T(1,128)} %domains.1, s32[1,1]{1,0:T(1,128)} %bitcast.4.lengths, bf16[1,512,1024]{2,1,0:T(8,128)(2,1)} %keys.1, bf16[1,512,1024]{2,1,0:T(8,128)(2,1)} %values.1, ...), custom_call_target="tpu_custom_call" | custom-call | tf_op jit(solution)/shard_map/pallas_call | solution.py:457
  37.0 0.7 %copy.14 = bf16[1,64,1024]{2,1,0:T(8,128)(2,1)} copy(bf16[1,64,1024]{2,1,0:T(8,128)(2,1)S(1)} %shard_map.118) | data formatting | bytes 262144
